TPU v7x, 32 devices: a whole 2x2x4 slice. The times are simulated.
32 devices in a mesh: groups: 2 (over x), blk: 16 (over z, y, core).
Axes of the slice: x: 2, y: 2, z: 4, core: 2. Of those that a mesh axis runs over, the one named last changes fastest.
Arguments:
- tokens: bfloat16 [8192, 8192], P(('groups', 'blk')), parts along dimension 0, may hold values from -6 to 6
- shrink_panels: bfloat16 [32, 8192, 64], P(None, 'blk'), may hold values from -0.0625 to 0.0625
- expand_panels: bfloat16 [32, 64, 8192], P(None, None, 'blk'), may hold values from -0.75 to 0.75
- adapter_scale: float32 [32], replicated, may hold values from 0.5 to 2
- block_adapter: int32 [128, 1], P('groups'), parts along dimension 0, may hold values from 0 to 31
- shard_counts: int32 [32], P('groups'), parts along dimension 0, may hold values from 1 to 256, as said below
Outputs:
- update: bfloat16 [8192, 8192], P(('groups', 'blk')), parts along dimension 0
There are 2 independent parts, one for each index of `groups`. A program takes and returns all parts, laid end to end along the dimension named above; an argument that names none is the same for every part. Nothing has to cross between parts.
Inputs may be any that keep to these rules, and one draw needn't show every extreme that they name: `shard_counts`: every shard holds at least one live row; in every draw some shard is full.
All inputs are finite; a program needn't handle non-finite values.
Results may differ from a plain program's by a relative error of at most 0.0049.
Values may be sent and summed in bfloat16 or wider, within the bound.
A program may use at most 128 MiB of HBM per device.

v0:
```python
import jax
import jax.numpy as jnp
from jax import lax
from jax.sharding import PartitionSpec as P

BLOCK = 64


def body(tokens, shrink_panels, expand_panels, adapter_scale, block_adapter, shard_counts):
    shard_rows, model_width = tokens.shape
    adapter_ids = block_adapter[:, 0]
    own_blocks = shard_rows // BLOCK
    shrink_sel = jnp.take(shrink_panels, adapter_ids, axis=0)
    expand_sel = jnp.take(expand_panels, adapter_ids, axis=0)
    blocked = tokens.reshape(own_blocks, BLOCK, model_width)
    down_maps = lax.all_to_all(shrink_sel, "blk", split_axis=0, concat_axis=1, tiled=True)
    up_maps = lax.all_to_all(expand_sel, "blk", split_axis=0, concat_axis=2, tiled=True)
    shard_index = lax.axis_index("blk")
    mine = lax.dynamic_slice_in_dim(adapter_ids, shard_index * own_blocks, own_blocks, 0)
    scales = jnp.take(adapter_scale, mine, axis=0)
    shrunk = jnp.einsum(
        "bkc,bcr->bkr", blocked, down_maps, preferred_element_type=jnp.float32
    ).astype(jnp.bfloat16)
    expanded = jnp.einsum("bkr,brc->bkc", shrunk, up_maps, preferred_element_type=jnp.float32)
    expanded = expanded * scales[:, None, None]
    own_count = lax.dynamic_index_in_dim(shard_counts, shard_index, 0, keepdims=False)
    within = lax.iota(jnp.int32, shard_rows)
    live_rows = (within < own_count).reshape(own_blocks, BLOCK, 1)
    masked_out = jnp.where(live_rows, expanded, 0.0).astype(jnp.bfloat16)
    return masked_out.reshape(shard_rows, model_width)


def solution(mesh):
    return jax.shard_map(
        body,
        mesh=mesh,
        in_specs=(
            P(("groups", "blk"), None),
            P(None, "blk", None),
            P(None, None, "blk"),
            P(),
            P("groups", None),
            P("groups"),
        ),
        out_specs=P(("groups", "blk"), None),
        check_vma=False,
    )
```

profile of v0, /device:TPU:15, one launch (start us, length us, event | category | flops | bytes accessed | tf_op | source)
XLA Modules:
  0.0 228.3 jit_solution(18072058476179573344)
XLA Ops:
  0.0 0.0 copy-start
  0.0 0.8 and_bitcast_fusion
  0.8 0.7 fusion.2
  1.5 0.1 copy-done
  1.6 2.8 %gather_fusion.1 = bf16[64,64,512]{2,1,0:T(8,128)(2,1)} fusion(bf16[32,64,512]{2,1,0:T(8,128)(2,1)S(1)} %copy-done, s32[1024]{0:T(1024)S(1)} %pad_clamp_fusion.1), kind=kCustom, calls=%fused_computation.1 | custom fusion | bytes 8388864 | tf_op jit(solution)/shard_map/jit(_take)/gather | solution.py:14
  4.4 4.6 %broadcast_select_fusion = bf16[64,64,512]{2,1,0:T(8,128)(2,1)} fusion(bf16[64,64,512]{2,1,0:T(8,128)(2,1)} %gather_fusion.1, pred[64]{0:T(512)(128)(4,1)S(1)} %and_bitcast_fusion), kind=kLoop, calls=%fused_computation.8 | loop fusion | flops 2097152 | bytes 8388672 | tf_op jit(solution)/shard_map/jit(_take)/select_n | solution.py:14
  9.1 6.5 %all-to-all-start.1 = ((bf16[64,64,512]{2,1,0:T(8,128)(2,1)}), bf16[64,64,512]{2,1,0:T(8,128)(2,1)}, u32[]{:S(2)}, u32[]{:S(2)}) async-start(bf16[64,64,512]{2,1,0:T(8,128)(2,1)} %broadcast_select_fusion), calls=%async_computation.1 | async-start | bytes 8388608 | tf_op jit(solution)/shard_map/all_to_all | solution.py:17
  15.6 4.4 %gather_fusion = bf16[64,512,64]{1,2,0:T(8,128)(2,1)} fusion(bf16[32,512,64]{1,2,0:T(8,128)(2,1)} %param.7, s32[1024]{0:T(1024)S(1)} %pad_clamp_fusion.1), kind=kCustom, calls=%fused_computation | custom fusion | bytes 8388864 | tf_op jit(solution)/shard_map/jit(_take)/gather | solution.py:13
  20.0 4.6 %broadcast_select_fusion.1 = bf16[64,512,64]{1,2,0:T(8,128)(2,1)} fusion(bf16[64,512,64]{1,2,0:T(8,128)(2,1)} %gather_fusion, pred[64]{0:T(512)(128)(4,1)S(1)} %and_bitcast_fusion), kind=kLoop, calls=%fused_computation.9 | loop fusion | flops 2097152 | bytes 8388672 | tf_op jit(solution)/shard_map/jit(_take)/select_n | solution.py:13
  24.6 0.0 copy-start.3
  24.6 0.0 copy-start.2
  24.6 0.0 copy-start.1
  24.6 83.5 %all-to-all-done.1 = bf16[64,64,512]{2,1,0:T(8,128)(2,1)} async-done(((bf16[64,64,512]{2,1,0:T(8,128)(2,1)}), bf16[64,64,512]{2,1,0:T(8,128)(2,1)}, u32[]{:S(2)}, u32[]{:S(2)}) %all-to-all-start.1) | async-done | bytes 4194336 | tf_op jit(solution)/shard_map/all_to_all | solution.py:17
  108.1 4.8 %all-to-all-start = ((bf16[64,512,64]{1,2,0:T(8,128)(2,1)}), bf16[64,512,64]{1,2,0:T(8,128)(2,1)}, u32[]{:S(2)}, u32[]{:S(2)}) async-start(bf16[64,512,64]{1,2,0:T(8,128)(2,1)} %broadcast_select_fusion.1), calls=%async_computation | async-start | bytes 8388608 | tf_op jit(solution)/shard_map/all_to_all | solution.py:16
  112.8 0.0 copy-done.3
  112.8 0.6 dynamic_slice.7
  113.4 0.0 copy-done.2
  113.4 0.1 fusion.3
  113.5 0.0 copy-done.1
  113.5 0.6 gather_fusion.2
  114.2 0.7 add_compare_fusion
  114.8 0.1 bitcast_select_fusion
  114.9 6.6 %copy.12 = bf16[16,4,64,512]{3,0,2,1:T(8,128)(2,1)} copy(bf16[16,4,64,512]{3,2,1,0:T(8,128)(2,1)} %bitcast.6) | data formatting | bytes 8388608 | tf_op jit(solution)/shard_map/all_to_all | solution.py:17
  121.5 7.4 %all_to_all.33 = bf16[4,64,8192]{2,1,0:T(8,128)(2,1)} reshape(bf16[4,64,16,512]{3,2,1,0:T(8,128)(2,1)} %bitcast.28) | data formatting | bytes 8388608 | tf_op jit(solution)/shard_map/all_to_all | solution.py:17
  128.9 76.4 %all-to-all-done = bf16[64,512,64]{1,2,0:T(8,128)(2,1)} async-done(((bf16[64,512,64]{1,2,0:T(8,128)(2,1)}), bf16[64,512,64]{1,2,0:T(8,128)(2,1)}, u32[]{:S(2)}, u32[]{:S(2)}) %all-to-all-start) | async-done | bytes 4194336 | tf_op jit(solution)/shard_map/all_to_all | solution.py:16
  205.3 6.6 %copy.13 = bf16[16,4,512,64]{2,0,3,1:T(8,128)(2,1)} copy(bf16[16,4,512,64]{2,3,1,0:T(8,128)(2,1)} %bitcast.3) | data formatting | bytes 8388608 | tf_op jit(solution)/shard_map/all_to_all | solution.py:16
  211.9 7.4 %all_to_all.29 = bf16[4,8192,64]{1,2,0:T(8,128)(2,1)} reshape(bf16[4,16,512,64]{2,1,3,0:T(8,128)(2,1)} %bitcast.29) | data formatting | bytes 8388608 | tf_op jit(solution)/shard_map/all_to_all | solution.py:16
  219.3 9.0 %fusion.1 = bf16[4,64,8192]{2,1,0:T(8,128)(2,1)} fusion(bf16[4,64,8192]{2,1,0:T(8,128)(2,1)} %all_to_all.33, f32[4]{0:T(128)S(1)} %bitcast_select_fusion, pred[4,64]{1,0:T(4,128)(4,1)S(1)} %add_compare_fusion, bf16[4,8192,64]{1,2,0:T(8,128)(2,1)} %all_to_all.29, bf16[4,64,8192]{2,1,0:T(8,128)(2,1)} %bitcast.30), kind=kOutput, calls=%fused_computation.5 | convolution fusion | flops 543178752 | bytes 16777488 | tf_op jit(solution)/shard_map/bkr,brc->bkc/dot_general | solution.py:24
  (2 shorter events, 0.0 us)
Async XLA Ops:
  0.0 1.6 copy-start
  9.1 99.0 %all-to-all-start.1 = ((bf16[64,64,512]{2,1,0:T(8,128)(2,1)}), bf16[64,64,512]{2,1,0:T(8,128)(2,1)}, u32[]{:S(2)}, u32[]{:S(2)}) async-start(bf16[64,64,512]{2,1,0:T(8,128)(2,1)} %broadcast_select_fusion), calls=%async_computation.1 | async-start | bytes 8388608 | tf_op jit(solution)/shard_map/all_to_all | solution.py:17
  24.6 88.3 %copy-start.3 = (s32[16]{0:T(128)S(1)}, s32[16]{0:T(128)}, u32[]{:S(2)}) copy-start(s32[16]{0:T(128)} %param.11) | copy-start | bytes 196
  24.6 88.9 %copy-start.2 = (s32[64,1]{0,1:T(1,128)S(1)}, s32[64,1]{0,1:T(1,128)}, u32[]{:S(2)}) copy-start(s32[64,1]{0,1:T(1,128)} %param.10) | copy-start | bytes 772
  24.6 89.0 %copy-start.1 = (f32[32]{0:T(128)S(1)}, f32[32]{0:T(128)}, u32[]{:S(2)}) copy-start(f32[32]{0:T(128)} %param.9) | copy-start | bytes 388
  108.1 97.2 %all-to-all-start = ((bf16[64,512,64]{1,2,0:T(8,128)(2,1)}), bf16[64,512,64]{1,2,0:T(8,128)(2,1)}, u32[]{:S(2)}, u32[]{:S(2)}) async-start(bf16[64,512,64]{1,2,0:T(8,128)(2,1)} %broadcast_select_fusion.1), calls=%async_computation | async-start | bytes 8388608 | tf_op jit(solution)/shard_map/all_to_all | solution.py:16
where the time goes:
time: 229 us; the launch traced here: 228 us
  waiting for transfers between devices  160 us (70%)
  local copies, waits for them, and re-layouts  36.5 us (16%)
  other arithmetic  11.5 us (5%)
  starting transfers between devices  11.3 us (5%)
  matrix products  9 us (4%)
    all_to_all x1, waiting for transfers between devices, body(): lax.all_to_all(expand_sel, 'blk', split_axis=0, concat_axis=2, tiled=True)  83.5 us
    all_to_all x1, waiting for transfers between devices, body(): lax.all_to_all(shrink_sel, 'blk', split_axis=0, concat_axis=1, tiled=True)  76.4 us
    all_to_all x2, local copies, waits for them, and re-layouts, body(): lax.all_to_all(shrink_sel, 'blk', split_axis=0, concat_axis=1, tiled=True)  14 us
    all_to_all x2, local copies, waits for them, and re-layouts, body(): lax.all_to_all(expand_sel, 'blk', split_axis=0, concat_axis=2, tiled=True)  14 us
    dot_general x1, matrix products, body(): jnp.einsum('bkr,brc->bkc', shrunk, up_maps, preferred_element_type=jnp.fl...  9 us
    all_to_all x1, starting transfers between devices, body(): lax.all_to_all(expand_sel, 'blk', split_axis=0, concat_axis=2, tiled=True)  6.52 us
    select_n x2, other arithmetic, body(): shrink_sel = jnp.take(shrink_panels, adapter_ids, axis=0)  5.25 us
    all_to_all x1, starting transfers between devices, body(): lax.all_to_all(shrink_sel, 'blk', split_axis=0, concat_axis=1, tiled=True)  4.78 us
  transfers between devices with their start and end apart: 2, of which 2 were waited for; matrix products, arithmetic and copies ran while one was open for 8% of the time, Pallas kernels for 0%

commit v1 on v0

v1 whole, which is shorter than its diff:
```python
import functools

import jax
import jax.numpy as jnp
from jax import lax
from jax.experimental import pallas as pl
from jax.experimental.pallas import tpu as pltpu
from jax.sharding import PartitionSpec as P

BLOCK = 64
CHUNKS = 4
MESH = pl.DeviceIdType.MESH


def kernel(
    n, groups,
    ids, scale, counts, tok_h, s_h, e_h, out_h,
    tok, ps, pe, rs, re, gs, ge, ss, se, acc, shr, out_v,
    loc, st_s, st_r, fw_s, fw_r, ax_s, ax_r, osem,
):
    g, me = lax.axis_index("groups"), lax.axis_index("blk")
    h = n // 2
    half, pos = me // h, me % h
    partner = (me + h) % n
    adapters, rank, feats = s_h.shape
    blocks = ss.shape[2]
    share = adapters // groups
    size = share // CHUNKS
    quarter = me // max(n // 4, 1)
    inner = jnp.logical_and(quarter >= 1, quarter <= 2)
    sources, own, other = (s_h, e_h), (ps, pe), (rs, re)
    sends, slots = (gs, ge), (ss, se)

    local = [
        pltpu.make_async_copy(s_h, ps, loc.at[0]),
        pltpu.make_async_copy(e_h, pe, loc.at[1]),
        pltpu.make_async_copy(tok_h, tok, loc.at[2]),
    ]
    for copy in local:
        copy.start()

    barrier = pltpu.get_barrier_semaphore()

    def greet(group, blk):
        pl.semaphore_signal(
            barrier, inc=1, device_id={"groups": group, "blk": blk}, device_id_type=MESH
        )

    greet(g, partner)
    for step in range(1, groups):
        greet((g + step) % groups, me)

    @pl.loop(1, h)
    def _(k):
        greet(g, half * h + (pos + k) % h)

    pl.semaphore_wait(barrier, 1 + (groups - 1) + (h - 1))

    def remote(src, dst, send_sem, recv_sem, group, blk):
        return pltpu.make_async_remote_copy(
            src_ref=src, dst_ref=dst, send_sem=send_sem, recv_sem=recv_sem,
            device_id={"groups": group, "blk": blk}, device_id_type=MESH,
        )

    def part(group, c):
        return pl.ds(group * share + c * size, size)

    def across(p, c):
        return remote(
            sources[p].at[part(g, c)], other[p].at[part(g, c)],
            st_s.at[p, c], st_r.at[p, c], g, partner,
        )

    def forward(p, c, step):
        return remote(
            other[p].at[part(g, c)], other[p].at[part(g, c)],
            fw_s.at[p, c, step - 1], fw_r.at[p, c, step - 1], (g + step) % groups, me,
        )

    def forwarded(p, c, step):
        rows = part((g - step + groups) % groups, c)
        return remote(
            other[p].at[rows], other[p].at[rows],
            fw_s.at[p, c, step - 1], fw_r.at[p, c, step - 1], (g + step) % groups, me,
        )

    def start_across():
        for p in range(2):
            for c in range(CHUNKS):
                across(p, c).start()

    def to_peer(f, p, d):
        return remote(
            sends[p].at[f, d], slots[p].at[f, pos],
            ax_s.at[f, p, d], ax_r.at[f, p, pos], g, half * h + d,
        )

    def from_peer(f, p, s):
        return remote(
            sends[p].at[f, s], slots[p].at[f, s],
            ax_s.at[f, p, s], ax_r.at[f, p, s], g, half * h + s,
        )

    def gather_and_send(f, p, panel):
        @pl.loop(1, h + 1)
        def _(k):
            d = (pos + k) % h
            for b in range(blocks):
                sends[p][f, d, b] = panel[ids[(half * h + d) * blocks + b]]

        @pl.loop(1, h)
        def _(k):
            to_peer(f, p, (pos + k) % h).start()

        for b in range(blocks):
            slots[p][f, pos, b] = sends[p][f, pos, b]

    @pl.when(inner)
    def _():
        start_across()

    for p in range(2):
        local[p].wait()
        gather_and_send(0, p, own[p])

    @pl.when(jnp.logical_not(inner))
    def _():
        start_across()

    for p in range(2):
        for c in range(CHUNKS):
            across(p, c).wait_recv()
            for step in range(1, groups):
                forward(p, c, step).start()
        for c in range(CHUNKS):
            for step in range(1, groups):
                forwarded(p, c, step).wait_recv()
        gather_and_send(1, p, other[p])

    local[2].wait()
    acc[...] = jnp.zeros_like(acc)

    def columns(f, s):
        owner = (half * (1 - f) + (1 - half) * f) * h + s
        return owner, pl.ds(pl.multiple_of(owner * feats, feats), feats)

    def shrink(f, s):
        _, cols = columns(f, s)
        for b in range(blocks):
            acc[b] += lax.dot_general(
                tok[b * BLOCK:(b + 1) * BLOCK, cols], ss[f, s, b],
                (((1,), (1,)), ((), ())), preferred_element_type=jnp.float32,
            )

    for f in range(2):
        shrink(f, pos)

        @pl.loop(1, h)
        def _(k):
            s = (pos - k + h) % h
            from_peer(f, 0, s).wait_recv()
            shrink(f, s)

    shr[...] = acc[...].astype(shr.dtype)
    count = counts[me]
    row = lax.broadcasted_iota(jnp.int32, (BLOCK, feats), 0)

    def put(owner, cols):
        return pltpu.make_async_copy(out_v.at[:, cols], out_h.at[:, cols], osem.at[owner])

    def expand(f, s):
        owner, cols = columns(f, s)
        for b in range(blocks):
            wide = jnp.dot(shr[b], se[f, s, b], preferred_element_type=jnp.float32)
            wide = wide * scale[ids[me * blocks + b]]
            live = row < count - b * BLOCK
            out_v[b * BLOCK:(b + 1) * BLOCK, cols] = jnp.where(live, wide, 0.0).astype(out_v.dtype)
        put(owner, cols).start()

    for f in range(2):
        expand(f, pos)

        @pl.loop(1, h)
        def _(k):
            s = (pos - k + h) % h
            from_peer(f, 1, s).wait_recv()
            expand(f, s)

    for p in range(2):
        for c in range(CHUNKS):
            across(p, c).wait_send()
            for step in range(1, groups):
                forward(p, c, step).wait_send()
        for f in range(2):
            @pl.loop(1, h)
            def _(k):
                to_peer(f, p, (pos + k) % h).wait_send()

    @pl.loop(0, n)
    def _(owner):
        put(owner, pl.ds(pl.multiple_of(owner * feats, feats), feats)).wait()


def body(n, groups, tokens, shrink_panels, expand_panels, adapter_scale, block_adapter, shard_counts):
    rows, width = tokens.shape
    adapters, feats, rank = shrink_panels.shape
    blocks = rows // BLOCK
    h = n // 2
    bf16 = tokens.dtype
    dma = pltpu.SemaphoreType.DMA
    smem = pl.BlockSpec(memory_space=pltpu.SMEM)
    hbm = pl.BlockSpec(memory_space=pl.ANY)
    panel = pltpu.VMEM((adapters, rank, feats), bf16)
    moved = pltpu.VMEM((2, h, blocks, rank, feats), bf16)
    return pl.pallas_call(
        functools.partial(kernel, n, groups),
        out_shape=jax.ShapeDtypeStruct((rows, width), bf16),
        in_specs=[smem, smem, smem, hbm, hbm, hbm],
        out_specs=hbm,
        scratch_shapes=[
            pltpu.VMEM((rows, width), bf16),
            panel, panel, panel, panel,
            moved, moved, moved, moved,
            pltpu.VMEM((blocks, BLOCK, rank), jnp.float32),
            pltpu.VMEM((blocks, BLOCK, rank), bf16),
            pltpu.VMEM((rows, width), bf16),
            dma((3,)),
            dma((2, CHUNKS)), dma((2, CHUNKS)),
            dma((2, CHUNKS, groups - 1)), dma((2, CHUNKS, groups - 1)),
            dma((2, 2, h)), dma((2, 2, h)),
            dma((n,)),
        ],
        compiler_params=pltpu.CompilerParams(
            collective_id=0, has_side_effects=True, vmem_limit_bytes=56 * 1024 * 1024
        ),
    )(
        block_adapter[:, 0], adapter_scale, shard_counts,
        tokens, jnp.swapaxes(shrink_panels, 1, 2), expand_panels,
    )


def solution(mesh):
    return jax.shard_map(
        functools.partial(body, mesh.shape["blk"], mesh.shape["groups"]),
        mesh=mesh,
        in_specs=(
            P(("groups", "blk"), None),
            P(None, "blk", None),
            P(None, None, "blk"),
            P(),
            P("groups", None),
            P("groups"),
        ),
        out_specs=P(("groups", "blk"), None),
        check_vma=False,
    )
```

time: 229 us -> 148 us (0.65)
  waiting for transfers between devices: 160 us -> 0 us
  Pallas kernels: 0 us -> 142 us
  local copies, waits for them, and re-layouts: 36.5 us -> 4.64 us
  other arithmetic: 11.5 us -> 0 us
  starting transfers between devices: 11.3 us -> 0 us
  matrix products: 9 us -> 0 us
    all_to_all x2 -> x0, waiting for transfers between devices: 160 us -> none  [the longest x1 83.5 us: body(): lax.all_to_all(expand_sel, 'blk', split_axis=0, concat_axis=2, tiled=True)]
    pallas_call x0 -> x1, Pallas kernels: none -> 142 us  [body(): pl.pallas_call(functools.partial(kernel, n, groups), out_shape=jax.ShapeD...]
    all_to_all x4 -> x0, local copies, waits for them, and re-layouts: 28 us -> none  [the longest x2 14 us: body(): lax.all_to_all(shrink_sel, 'blk', split_axis=0, concat_axis=1, tiled=True)]
    all_to_all x2 -> x0, starting transfers between devices: 11.3 us -> none  [the longest x1 6.52 us: body(): lax.all_to_all(expand_sel, 'blk', split_axis=0, concat_axis=2, tiled=True)]
    select_n x5 -> x0, other arithmetic: 10 us -> none  [the longest x2 5.25 us: body(): shrink_sel = jnp.take(shrink_panels, adapter_ids, axis=0)]
    dot_general x1 -> x0, matrix products: 9 us -> none  [body(): jnp.einsum('bkr,brc->bkc', shrunk, up_maps, preferred_element_type=jnp.fl...]
    gather x3 -> x0, local copies, waits for them, and re-layouts: 7.83 us -> none  [the longest x1 4.37 us: body(): shrink_sel = jnp.take(shrink_panels, adapter_ids, axis=0)]
    unnamed x8 -> x1, local copies, waits for them, and re-layouts: 0.14 us -> 4.64 us
  transfers between devices with their start and end apart: 2 -> 0, of which waited for: 2 -> 0; matrix products, arithmetic and copies ran while one was open for 8% -> 0% of each run, Pallas kernels for 0% -> 0%
where the time goes in v1:
time: 148 us; the launch traced here: 146 us
  Pallas kernels  142 us (96%)
  local copies, waits for them, and re-layouts  4.64 us (3%)
    pallas_call x1, Pallas kernels, body(): pl.pallas_call(functools.partial(kernel, n, groups), out_shape=jax.ShapeD...  142 us
    unnamed x1, local copies, waits for them, and re-layouts  4.64 us

profile of v1, /device:TPU:15, one launch (start us, length us, event | category | flops | bytes accessed | tf_op | source)
XLA Modules:
  0.0 146.4 jit_solution(15030578694092171809)
XLA Ops:
  0.0 141.8 %shard_map.64 = bf16[256,8192]{1,0:T(8,128)(2,1)} custom-call(s32[64]{0:T(128)} %bitcast.3, f32[32]{0:T(128)} %scale.1, s32[16]{0:T(128)} %counts.1, bf16[256,8192]{1,0:T(8,128)(2,1)} %tok_h.1, bf16[32,64,512]{2,1,0:T(8,128)(2,1)} %bitcast.2, bf16[32,64,512]{2,1,0:T(8,128)(2,1)} %e_h.1), custom_call_target="tpu_custom_call" | custom-call | tf_op jit(solution)/shard_map/pallas_call | solution.py:215
  141.8 4.6 %copy.8 = bf16[256,8192]{1,0:T(8,128)(2,1)} copy(bf16[256,8192]{1,0:T(8,128)(2,1)} %shard_map.64) | data formatting | bytes 8388608

commit v2 on v1

v2 whole, which is shorter than its diff:
```python
import functools

import jax
import jax.numpy as jnp
from jax import lax
from jax.experimental import pallas as pl
from jax.experimental.pallas import tpu as pltpu
from jax.sharding import PartitionSpec as P

BLOCK = 64
CHUNKS = 4
MESH = pl.DeviceIdType.MESH


def kernel(
    n, groups,
    ids, scale, counts, tok_h, s_h, e_h, out_h,
    tok, ps, pe, rs0, re0, rs1, re1, gs, ge, fs, fe, ss, se, guest, psum, pgot, acc, shr, out_v,
    loc, st_s, st_r, fw_s, fw_r, ax_s, ax_r, fx_s, tk_s, tk_r, pt_s, pt_r, osem,
):
    g, me = lax.axis_index("groups"), lax.axis_index("blk")
    h, w = n // 2, n // 4
    half, pos, q, u = me // h, me % h, me // w, me % w
    adapters, rank, feats = s_h.shape
    blocks = ss.shape[1]
    share = adapters // groups
    size = share // CHUNKS
    near_inner, near_outer = 1 + half, 3 * half
    far = (2 - half, 3 - 3 * half)
    inside = half * (3 - q) + (1 - half) * q
    inner, outer = inside == 1, inside == 0
    sources, own = (s_h, e_h), (ps, pe)
    others = ((rs0, re0), (rs1, re1))
    sends, far_sends, slots = (gs, ge), (fs, fe), (ss, se)

    local = [
        pltpu.make_async_copy(s_h, ps, loc.at[0]),
        pltpu.make_async_copy(e_h, pe, loc.at[1]),
        pltpu.make_async_copy(tok_h, tok, loc.at[2]),
    ]
    for copy in local:
        copy.start()

    barrier = pltpu.get_barrier_semaphore()

    def greet(group, blk):
        pl.semaphore_signal(
            barrier, inc=1, device_id={"groups": group, "blk": blk}, device_id_type=MESH
        )

    for quarter in far:
        greet(g, quarter * w + u)
    for step in range(1, groups):
        greet((g + step) % groups, me)

    @pl.loop(1, h)
    def _(k):
        greet(g, half * h + (pos + k) % h)

    pl.semaphore_wait(barrier, 2 + (groups - 1) + (h - 1))

    def remote(src, dst, send_sem, recv_sem, group, blk):
        return pltpu.make_async_remote_copy(
            src_ref=src, dst_ref=dst, send_sem=send_sem, recv_sem=recv_sem,
            device_id={"groups": group, "blk": blk}, device_id_type=MESH,
        )

    def part(group, c):
        return pl.ds(group * share + c * size, size)

    def across(j, p, c):
        return remote(
            sources[p].at[part(g, c)], others[j][p].at[part(g, c)],
            st_s.at[p, c], st_r.at[j, p, c], g, far[0] * w + u,
        )

    def forward(j, p, c, step):
        rows = others[j][p].at[part(g, c)]
        sem = (j, p, c, step - 1)
        return remote(rows, rows, fw_s.at[sem], fw_r.at[sem], (g + step) % groups, me)

    def forwarded(j, p, c, step):
        rows = others[j][p].at[part((g - step + groups) % groups, c)]
        sem = (j, p, c, step - 1)
        return remote(rows, rows, fw_s.at[sem], fw_r.at[sem], (g + step) % groups, me)

    def start_across(j):
        for p in range(2):
            for c in range(CHUNKS):
                across(j, p, c).start()

    def to_peer(p, d):
        return remote(
            sends[p].at[d], slots[p].at[me], ax_s.at[p, d], ax_r.at[p, me], g, half * h + d
        )

    def to_far_peer(j, p, d):
        owner = far[j] * w + u
        return remote(
            far_sends[p].at[j, d], slots[p].at[owner],
            fx_s.at[j, p, d], ax_r.at[p, owner], g, half * h + d,
        )

    def from_owner(p, owner):
        return remote(
            slots[p].at[owner], slots[p].at[owner], ax_s.at[p, 0], ax_r.at[p, owner], g, me
        )

    def near_send(p):
        local[p].wait()

        @pl.loop(1, h + 1)
        def _(k):
            d = (pos + k) % h
            for b in range(blocks):
                sends[p][d, b] = own[p][ids[(half * h + d) * blocks + b]]

        @pl.loop(1, h)
        def _(k):
            to_peer(p, (pos + k) % h).start()

        for b in range(blocks):
            slots[p][me, b] = sends[p][pos, b]

    def end_at(k):
        return (near_outer - 2 * half) * w + (u + k) % w

    def side_at(k):
        return (q - 2 * half) * w + (u + k) % w

    def far_send(j, p):
        panel = others[j][p]

        def pick(d):
            for b in range(blocks):
                far_sends[p][j, d, b] = panel[ids[(half * h + d) * blocks + b]]

        if p == 1 or j == 1:
            @pl.loop(0, w)
            def _(k):
                pick(end_at(k))

            @pl.loop(0, w)
            def _(k):
                to_far_peer(j, p, end_at(k)).start()

        @pl.loop(1, w + 1)
        def _(k):
            pick(side_at(k))

        @pl.loop(1, w)
        def _(k):
            to_far_peer(j, p, side_at(k)).start()

        for b in range(blocks):
            slots[p][far[j] * w + u, b] = far_sends[p][j, side_at(0), b]

    def columns(owner):
        return pl.ds(pl.multiple_of(owner * feats, feats), feats)

    def visit(k):
        v = (u + k) % w
        return remote(
            tok_h.at[:, columns(far[0] * w + v)], guest.at[u],
            tk_s.at[v], tk_r.at[u], g, near_inner * w + v,
        )

    def visited(v):
        return remote(guest.at[v], guest.at[v], tk_s.at[v], tk_r.at[v], g, me)

    def back(v):
        return remote(psum.at[v], pgot.at[u], pt_s.at[v], pt_r.at[u], g, near_outer * w + v)

    def came_back(v):
        return remote(pgot.at[v], pgot.at[v], pt_s.at[v], pt_r.at[v], g, me)

    def down(rows, panel):
        return lax.dot_general(
            rows, panel, (((1,), (1,)), ((), ())), preferred_element_type=jnp.float32
        )

    @pl.when(inner)
    def _():
        start_across(0)
        for p in range(2):
            near_send(p)
        for j in range(2):
            for p in range(2):
                for c in range(CHUNKS):
                    across(j, p, c).wait_recv()
                    for step in range(1, groups):
                        forward(j, p, c, step).start()
                for c in range(CHUNKS):
                    for step in range(1, groups):
                        forwarded(j, p, c, step).wait_recv()
                far_send(j, p)
                if j == 0 and p == 0:
                    @pl.loop(0, w)
                    def _(k):
                        v = (u + k) % w
                        visited(v).wait_recv()
                        for b in range(blocks):
                            panel = rs0[ids[(near_outer * w + v) * blocks + b]]
                            rows = guest[v, b * BLOCK:(b + 1) * BLOCK, :]
                            at = (b % 2) * rank
                            psum[v, b // 2, :, at:at + rank] = down(rows, panel)

                    @pl.loop(0, w)
                    def _(k):
                        back((u + k) % w).start()

    @pl.when(outer)
    def _():
        @pl.loop(0, w)
        def _(k):
            visit(k).start()

        near_send(0)
        start_across(1)
        near_send(1)

    local[2].wait()
    acc[...] = jnp.zeros_like(acc)
    order = (
        q,
        inside * far[0] + (1 - inside) * near_inner,
        inside * far[1] + (1 - inside) * far[0],
        inside * near_outer + (1 - inside) * far[1],
    )

    def each(p, turn, use):
        @pl.loop(0, w)
        def _(k):
            owner = order[turn] * w + (u - k + w) % w
            absent = k > 0
            if turn in (1, 2):
                absent = jnp.logical_or(absent, outer)
            if turn == 3:
                absent = k >= 0

            @pl.when(absent)
            def _():
                from_owner(p, owner).wait_recv()

            use(owner)

    def shrink(owner):
        for b in range(blocks):
            acc[b] += down(tok[b * BLOCK:(b + 1) * BLOCK, columns(owner)], ss[owner, b])

    for turn in range(4):
        if turn != 2:
            each(0, turn, shrink)
            continue

        @pl.when(inner)
        def _():
            each(0, 2, shrink)

        @pl.when(outer)
        def _():
            @pl.loop(0, w)
            def _(k):
                v = (u - k + w) % w
                came_back(v).wait_recv()
                for b in range(blocks):
                    at = (b % 2) * rank
                    acc[b] += pgot[v, b // 2, :, at:at + rank]

    shr[...] = acc[...].astype(shr.dtype)
    count = counts[me]
    row = lax.broadcasted_iota(jnp.int32, (BLOCK, feats), 0)

    def put(owner):
        cols = columns(owner)
        return pltpu.make_async_copy(out_v.at[:, cols], out_h.at[:, cols], osem.at[owner])

    def expand(owner):
        for b in range(blocks):
            wide = jnp.dot(shr[b], se[owner, b], preferred_element_type=jnp.float32)
            wide = wide * scale[ids[me * blocks + b]]
            live = row < count - b * BLOCK
            out_v[b * BLOCK:(b + 1) * BLOCK, columns(owner)] = jnp.where(
                live, wide, 0.0
            ).astype(out_v.dtype)
        put(owner).start()

    for turn in range(4):
        each(1, turn, expand)

    for p in range(2):
        for c in range(CHUNKS):
            across(0, p, c).wait_send()

        @pl.loop(1, h)
        def _(k):
            to_peer(p, (pos + k) % h).wait_send()

    @pl.when(inner)
    def _():
        for j in range(2):
            for p in range(2):
                for c in range(CHUNKS):
                    for step in range(1, groups):
                        forward(j, p, c, step).wait_send()

                @pl.loop(1, w)
                def _(k):
                    to_far_peer(j, p, side_at(k)).wait_send()

                if p == 1 or j == 1:
                    @pl.loop(0, w)
                    def _(k):
                        to_far_peer(j, p, end_at(k)).wait_send()

        @pl.loop(0, w)
        def _(k):
            back((u + k) % w).wait_send()

    @pl.when(outer)
    def _():
        @pl.loop(0, w)
        def _(k):
            visit(k).wait_send()

    @pl.loop(0, n)
    def _(owner):
        put(owner).wait()


def body(n, groups, tokens, shrink_panels, expand_panels, adapter_scale, block_adapter, shard_counts):
    rows, width = tokens.shape
    adapters, feats, rank = shrink_panels.shape
    blocks = rows // BLOCK
    h, w = n // 2, n // 4
    bf16 = tokens.dtype
    dma = pltpu.SemaphoreType.DMA
    smem = pl.BlockSpec(memory_space=pltpu.SMEM)
    hbm = pl.BlockSpec(memory_space=pl.ANY)
    panel = pltpu.VMEM((adapters, rank, feats), bf16)
    near = pltpu.VMEM((h, blocks, rank, feats), bf16)
    distant = pltpu.VMEM((2, h, blocks, rank, feats), bf16)
    slot = pltpu.VMEM((n, blocks, rank, feats), bf16)
    sums = pltpu.VMEM((w, (blocks + 1) // 2, BLOCK, 2 * rank), jnp.float32)
    return pl.pallas_call(
        functools.partial(kernel, n, groups),
        out_shape=jax.ShapeDtypeStruct((rows, width), bf16),
        in_specs=[smem, smem, smem, hbm, hbm, hbm],
        out_specs=hbm,
        scratch_shapes=[
            pltpu.VMEM((rows, width), bf16),
            panel, panel, panel, panel, panel, panel,
            near, near, distant, distant, slot, slot,
            pltpu.VMEM((w, rows, feats), bf16),
            sums, sums,
            pltpu.VMEM((blocks, BLOCK, rank), jnp.float32),
            pltpu.VMEM((blocks, BLOCK, rank), bf16),
            pltpu.VMEM((rows, width), bf16),
            dma((3,)),
            dma((2, CHUNKS)), dma((2, 2, CHUNKS)),
            dma((2, 2, CHUNKS, groups - 1)), dma((2, 2, CHUNKS, groups - 1)),
            dma((2, h)), dma((2, n)), dma((2, 2, h)),
            dma((w,)), dma((w,)), dma((w,)), dma((w,)),
            dma((n,)),
        ],
        compiler_params=pltpu.CompilerParams(
            collective_id=0, has_side_effects=True, vmem_limit_bytes=60 * 1024 * 1024
        ),
    )(
        block_adapter[:, 0], adapter_scale, shard_counts,
        tokens, jnp.swapaxes(shrink_panels, 1, 2), expand_panels,
    )


def solution(mesh):
    return jax.shard_map(
        functools.partial(body, mesh.shape["blk"], mesh.shape["groups"]),
        mesh=mesh,
        in_specs=(
            P(("groups", "blk"), None),
            P(None, "blk", None),
            P(None, None, "blk"),
            P(),
            P("groups", None),
            P("groups"),
        ),
        out_specs=P(("groups", "blk"), None),
        check_vma=False,
    )
```

time: 148 us -> 137 us (0.926)
  Pallas kernels: 142 us -> 131 us
    pallas_call x1, Pallas kernels: 142 us -> 131 us  [body(): pl.pallas_call(functools.partial(kernel, n, groups), out_shape=jax.ShapeD...]
where the time goes in v2:
time: 137 us; the launch traced here: 135 us
  Pallas kernels  131 us (96%)
  local copies, waits for them, and re-layouts  4.64 us (3%)
    pallas_call x1, Pallas kernels, body(): pl.pallas_call(functools.partial(kernel, n, groups), out_shape=jax.ShapeD...  131 us
    unnamed x1, local copies, waits for them, and re-layouts  4.64 us

profile of v2, /device:TPU:15, one launch (start us, length us, event | category | flops | bytes accessed | tf_op | source)
XLA Modules:
  0.0 135.5 jit_solution(705138442029879950)
XLA Ops:
  0.0 130.8 %shard_map.64 = bf16[256,8192]{1,0:T(8,128)(2,1)} custom-call(s32[64]{0:T(128)} %bitcast.3, f32[32]{0:T(128)} %scale.1, s32[16]{0:T(128)} %counts.1, bf16[256,8192]{1,0:T(8,128)(2,1)} %tok_h.1, bf16[32,64,512]{2,1,0:T(8,128)(2,1)} %bitcast.2, bf16[32,64,512]{2,1,0:T(8,128)(2,1)} %e_h.1), custom_call_target="tpu_custom_call" | custom-call | tf_op jit(solution)/shard_map/pallas_call | solution.py:345
  130.8 4.6 %copy.8 = bf16[256,8192]{1,0:T(8,128)(2,1)} copy(bf16[256,8192]{1,0:T(8,128)(2,1)} %shard_map.64) | data formatting | bytes 8388608

commit v3 on v2

v3 whole, which is shorter than its diff:
```python
import functools

import jax
import jax.numpy as jnp
from jax import lax
from jax.experimental import pallas as pl
from jax.experimental.pallas import tpu as pltpu
from jax.sharding import PartitionSpec as P

BLOCK = 64
CHUNKS = 2
SLICES = 2
MESH = pl.DeviceIdType.MESH


def kernel(
    n, groups,
    ids, scale, counts, tok_h, s_h, e_h, out_h,
    tok, ps, pe, gs, ge, fs, fe, ss, se, guest, psum, pgot, acc, shr, out_v,
    loc, st_s, st_r, fw_s, fw_r, ax_s, ax_r, fx_s, fx_r, tk_s, tk_r, pt_s, pt_r, osem, *distant,
):
    g, me = lax.axis_index("groups"), lax.axis_index("blk")
    h, w = n // 2, n // 4
    half, pos, q, u = me // h, me % h, me // w, me % w
    adapters, rank, feats = s_h.shape
    blocks = ss.shape[2]
    thick = rank // SLICES
    share = adapters // groups
    size = share // CHUNKS
    near_inner, near_outer = 1 + half, 3 * half
    far = (2 - half, 3 - 3 * half)
    inside = half * (3 - q) + (1 - half) * q
    inner, outer = inside == 1, inside == 0
    sources, own = (s_h, e_h), (ps, pe)
    others = [
        [distant[(2 * j + p) * SLICES:(2 * j + p + 1) * SLICES] for p in range(2)]
        for j in range(2)
    ]
    sends, far_sends, slots = (gs, ge), (fs, fe), (ss, se)

    local = [
        pltpu.make_async_copy(s_h, ps, loc.at[0]),
        pltpu.make_async_copy(e_h, pe, loc.at[1]),
        pltpu.make_async_copy(tok_h, tok, loc.at[2]),
    ]
    for copy in local:
        copy.start()

    barrier = pltpu.get_barrier_semaphore()

    def greet(group, blk):
        pl.semaphore_signal(
            barrier, inc=1, device_id={"groups": group, "blk": blk}, device_id_type=MESH
        )

    for quarter in far:
        greet(g, quarter * w + u)
    for step in range(1, groups):
        greet((g + step) % groups, me)

    @pl.loop(1, h)
    def _(k):
        greet(g, half * h + (pos + k) % h)

    pl.semaphore_wait(barrier, 2 + (groups - 1) + (h - 1))

    def remote(src, dst, send_sem, recv_sem, group, blk):
        return pltpu.make_async_remote_copy(
            src_ref=src, dst_ref=dst, send_sem=send_sem, recv_sem=recv_sem,
            device_id={"groups": group, "blk": blk}, device_id_type=MESH,
        )

    def part(group, c):
        return pl.ds(group * share + c * size, size)

    def ranks(r):
        return pl.ds(r * thick, thick)

    def across(j, p, r, c):
        return remote(
            sources[p].at[part(g, c), ranks(r)], others[j][p][r].at[part(g, c)],
            st_s.at[p, r, c], st_r.at[j, p, r, c], g, far[0] * w + u,
        )

    def forward(j, p, r, c, step):
        rows = others[j][p][r].at[part(g, c)]
        sem = (j, p, r, c, step - 1)
        return remote(rows, rows, fw_s.at[sem], fw_r.at[sem], (g + step) % groups, me)

    def forwarded(j, p, r, c, step):
        rows = others[j][p][r].at[part((g - step + groups) % groups, c)]
        sem = (j, p, r, c, step - 1)
        return remote(rows, rows, fw_s.at[sem], fw_r.at[sem], (g + step) % groups, me)

    def start_across(j, p):
        for r in range(SLICES):
            for c in range(CHUNKS):
                across(j, p, r, c).start()

    def to_peer(p, d):
        return remote(
            sends[p].at[d], slots[p].at[me], ax_s.at[p, d], ax_r.at[p, me], g, half * h + d
        )

    def to_far_peer(j, p, r, d):
        owner = far[j] * w + u
        return remote(
            far_sends[p].at[j, d, r], slots[p].at[owner, r],
            fx_s.at[j, p, r, d], fx_r.at[j, p, r, u], g, half * h + d,
        )

    def from_near(p, owner):
        rows = slots[p].at[owner]
        return remote(rows, rows, ax_s.at[p, 0], ax_r.at[p, owner], g, me)

    def from_far(j, p, r, v):
        rows = slots[p].at[far[j] * w + v, r]
        return remote(rows, rows, fx_s.at[j, p, r, 0], fx_r.at[j, p, r, v], g, me)

    def near_send(p):
        local[p].wait()

        @pl.loop(1, h + 1)
        def _(k):
            d = (pos + k) % h
            for b in range(blocks):
                panel = own[p][ids[(half * h + d) * blocks + b]]
                for r in range(SLICES):
                    sends[p][d, r, b] = panel[r * thick:(r + 1) * thick]

        @pl.loop(1, h)
        def _(k):
            to_peer(p, (pos + k) % h).start()

        slots[p][me] = sends[p][pos]

    def end_at(k):
        return (near_outer - 2 * half) * w + (u + k) % w

    def side_at(k):
        return (q - 2 * half) * w + (u + k) % w

    def far_send(j, p, r):
        panel = others[j][p][r]

        def pick(d):
            for b in range(blocks):
                far_sends[p][j, d, r, b] = panel[ids[(half * h + d) * blocks + b]]

        if p == 1 or j == 1:
            @pl.loop(0, w)
            def _(k):
                pick(end_at(k))

            @pl.loop(0, w)
            def _(k):
                to_far_peer(j, p, r, end_at(k)).start()

        @pl.loop(1, w + 1)
        def _(k):
            pick(side_at(k))

        @pl.loop(1, w)
        def _(k):
            to_far_peer(j, p, r, side_at(k)).start()

        slots[p][far[j] * w + u, r] = far_sends[p][j, side_at(0), r]

    def columns(owner):
        return pl.ds(pl.multiple_of(owner * feats, feats), feats)

    def visit(k):
        v = (u + k) % w
        return remote(
            tok_h.at[:, columns(far[0] * w + v)], guest.at[u],
            tk_s.at[v], tk_r.at[u], g, near_inner * w + v,
        )

    def visited(v):
        return remote(guest.at[v], guest.at[v], tk_s.at[v], tk_r.at[v], g, me)

    def back(v):
        return remote(psum.at[v], pgot.at[u], pt_s.at[v], pt_r.at[u], g, near_outer * w + v)

    def came_back(v):
        return remote(pgot.at[v], pgot.at[v], pt_s.at[v], pt_r.at[v], g, me)

    def down(rows, panel):
        return lax.dot_general(
            rows, panel, (((1,), (1,)), ((), ())), preferred_element_type=jnp.float32
        )

    @pl.when(inner)
    def _():
        for p in range(2):
            start_across(0, p)
        for p in range(2):
            near_send(p)
        for j, p, r in [(j, p, r) for j in range(2) for p in range(2) for r in range(SLICES)]:
            for c in range(CHUNKS):
                across(j, p, r, c).wait_recv()
                for step in range(1, groups):
                    forward(j, p, r, c, step).start()
            for c in range(CHUNKS):
                for step in range(1, groups):
                    forwarded(j, p, r, c, step).wait_recv()
            far_send(j, p, r)
            if (j, p, r) == (0, 0, SLICES - 1):
                @pl.loop(0, w)
                def _(k):
                    v = (u + k) % w
                    visited(v).wait_recv()
                    for b in range(blocks):
                        rows = guest[v, b * BLOCK:(b + 1) * BLOCK, :]
                        for i in range(SLICES):
                            panel = others[0][0][i][ids[(near_outer * w + v) * blocks + b]]
                            at = (b % 2) * rank + i * thick
                            psum[v, b // 2, :, at:at + thick] = down(rows, panel)

                @pl.loop(0, w)
                def _(k):
                    back((u + k) % w).start()

    @pl.when(outer)
    def _():
        @pl.loop(0, w)
        def _(k):
            visit(k).start()

        near_send(0)
        start_across(1, 0)
        start_across(1, 1)
        near_send(1)

    local[2].wait()
    acc[...] = jnp.zeros_like(acc)
    def each(p, quarter, j, k0, use):
        @pl.loop(0, w)
        def _(k):
            v = (u - k + w) % w

            @pl.when(k >= k0)
            def _():
                if j is None:
                    from_near(p, quarter * w + v).wait_recv()
                else:
                    for r in range(SLICES):
                        from_far(j, p, r, v).wait_recv()

            use(quarter * w + v)

    def panel_of(slot, owner, b):
        return jnp.concatenate([slot[owner, r, b] for r in range(SLICES)], axis=0)

    def shrink(owner):
        for b in range(blocks):
            acc[b] += down(tok[b * BLOCK:(b + 1) * BLOCK, columns(owner)], panel_of(ss, owner, b))

    each(0, q, None, 1, shrink)

    @pl.when(inner)
    def _():
        for j in range(2):
            each(0, far[j], j, 1, shrink)
        each(0, near_outer, None, 0, shrink)

    @pl.when(outer)
    def _():
        each(0, near_inner, None, 0, shrink)

        @pl.loop(0, w)
        def _(k):
            v = (u - k + w) % w
            came_back(v).wait_recv()
            for b in range(blocks):
                at = (b % 2) * rank
                acc[b] += pgot[v, b // 2, :, at:at + rank]

        each(0, far[1], 1, 0, shrink)

    shr[...] = acc[...].astype(shr.dtype)
    count = counts[me]
    row = lax.broadcasted_iota(jnp.int32, (BLOCK, feats), 0)

    def put(owner):
        cols = columns(owner)
        return pltpu.make_async_copy(out_v.at[:, cols], out_h.at[:, cols], osem.at[owner])

    def expand(owner):
        for b in range(blocks):
            wide = jnp.dot(shr[b], panel_of(se, owner, b), preferred_element_type=jnp.float32)
            wide = wide * scale[ids[me * blocks + b]]
            live = row < count - b * BLOCK
            out_v[b * BLOCK:(b + 1) * BLOCK, columns(owner)] = jnp.where(
                live, wide, 0.0
            ).astype(out_v.dtype)
        put(owner).start()

    each(1, q, None, 1, expand)

    @pl.when(inner)
    def _():
        for j in range(2):
            each(1, far[j], j, 1, expand)
        each(1, near_outer, None, 0, expand)

    @pl.when(outer)
    def _():
        each(1, near_inner, None, 0, expand)
        for j in range(2):
            each(1, far[j], j, 0, expand)

    for p in range(2):
        for r in range(SLICES):
            for c in range(CHUNKS):
                across(0, p, r, c).wait_send()

        @pl.loop(1, h)
        def _(k):
            to_peer(p, (pos + k) % h).wait_send()

    @pl.when(inner)
    def _():
        for j, p, r in [(j, p, r) for j in range(2) for p in range(2) for r in range(SLICES)]:
            for c in range(CHUNKS):
                for step in range(1, groups):
                    forward(j, p, r, c, step).wait_send()

            @pl.loop(1, w)
            def _(k):
                to_far_peer(j, p, r, side_at(k)).wait_send()

            if p == 1 or j == 1:
                @pl.loop(0, w)
                def _(k):
                    to_far_peer(j, p, r, end_at(k)).wait_send()

        @pl.loop(0, w)
        def _(k):
            back((u + k) % w).wait_send()

    @pl.when(outer)
    def _():
        @pl.loop(0, w)
        def _(k):
            visit(k).wait_send()

    @pl.loop(0, n)
    def _(owner):
        put(owner).wait()


def body(n, groups, tokens, shrink_panels, expand_panels, adapter_scale, block_adapter, shard_counts):
    rows, width = tokens.shape
    adapters, feats, rank = shrink_panels.shape
    blocks = rows // BLOCK
    h, w = n // 2, n // 4
    bf16 = tokens.dtype
    dma = pltpu.SemaphoreType.DMA
    smem = pl.BlockSpec(memory_space=pltpu.SMEM)
    hbm = pl.BlockSpec(memory_space=pl.ANY)
    panel = pltpu.VMEM((adapters, rank, feats), bf16)
    slice_of = pltpu.VMEM((adapters, rank // SLICES, feats), bf16)
    moved = (SLICES, blocks, rank // SLICES, feats)
    near = pltpu.VMEM((h, *moved), bf16)
    distant = pltpu.VMEM((2, h, *moved), bf16)
    slot = pltpu.VMEM((n, *moved), bf16)
    sums = pltpu.VMEM((w, (blocks + 1) // 2, BLOCK, 2 * rank), jnp.float32)
    return pl.pallas_call(
        functools.partial(kernel, n, groups),
        out_shape=jax.ShapeDtypeStruct((rows, width), bf16),
        in_specs=[smem, smem, smem, hbm, hbm, hbm],
        out_specs=hbm,
        scratch_shapes=[
            pltpu.VMEM((rows, width), bf16),
            panel, panel,
            near, near, distant, distant, slot, slot,
            pltpu.VMEM((w, rows, feats), bf16),
            sums, sums,
            pltpu.VMEM((blocks, BLOCK, rank), jnp.float32),
            pltpu.VMEM((blocks, BLOCK, rank), bf16),
            pltpu.VMEM((rows, width), bf16),
            dma((3,)),
            dma((2, SLICES, CHUNKS)), dma((2, 2, SLICES, CHUNKS)),
            dma((2, 2, SLICES, CHUNKS, groups - 1)), dma((2, 2, SLICES, CHUNKS, groups - 1)),
            dma((2, h)), dma((2, n)), dma((2, 2, SLICES, h)), dma((2, 2, SLICES, w)),
            dma((w,)), dma((w,)), dma((w,)), dma((w,)),
            dma((n,)),
            *[slice_of] * (4 * SLICES),
        ],
        compiler_params=pltpu.CompilerParams(
            collective_id=0, has_side_effects=True, vmem_limit_bytes=60 * 1024 * 1024
        ),
    )(
        block_adapter[:, 0], adapter_scale, shard_counts,
        tokens, jnp.swapaxes(shrink_panels, 1, 2), expand_panels,
    )


def solution(mesh):
    return jax.shard_map(
        functools.partial(body, mesh.shape["blk"], mesh.shape["groups"]),
        mesh=mesh,
        in_specs=(
            P(("groups", "blk"), None),
            P(None, "blk", None),
            P(None, None, "blk"),
            P(),
            P("groups", None),
            P("groups"),
        ),
        out_specs=P(("groups", "blk"), None),
        check_vma=False,
    )
```

time: 137 us -> 133 us (0.971)
  Pallas kernels: 131 us -> 126 us
    pallas_call x1, Pallas kernels: 131 us -> 126 us  [body(): pl.pallas_call(functools.partial(kernel, n, groups), out_shape=jax.ShapeD...]
where the time goes in v3:
time: 133 us; the launch traced here: 131 us
  Pallas kernels  126 us (95%)
  local copies, waits for them, and re-layouts  4.64 us (3%)
    pallas_call x1, Pallas kernels, body(): pl.pallas_call(functools.partial(kernel, n, groups), out_shape=jax.ShapeD...  126 us
    unnamed x1, local copies, waits for them, and re-layouts  4.64 us

profile of v3, /device:TPU:15, one launch (start us, length us, event | category | flops | bytes accessed | tf_op | source)
XLA Modules:
  0.0 130.9 jit_solution(18246567106122502625)
XLA Ops:
  0.0 126.2 %shard_map.64 = bf16[256,8192]{1,0:T(8,128)(2,1)} custom-call(s32[64]{0:T(128)} %bitcast.3, f32[32]{0:T(128)} %scale.1, s32[16]{0:T(128)} %counts.1, bf16[256,8192]{1,0:T(8,128)(2,1)} %tok_h.1, bf16[32,64,512]{2,1,0:T(8,128)(2,1)} %bitcast.2, bf16[32,64,512]{2,1,0:T(8,128)(2,1)} %e_h.1), custom_call_target="tpu_custom_call" | custom-call | tf_op jit(solution)/shard_map/pallas_call | solution.py:369
  126.2 4.6 %copy.8 = bf16[256,8192]{1,0:T(8,128)(2,1)} copy(bf16[256,8192]{1,0:T(8,128)(2,1)} %shard_map.64) | data formatting | bytes 8388608
